TPU v7x, 256 devices: a whole 4x4x8 slice. The times are simulated.
256 devices in a mesh: grp: 8 (over z), ord: 32 (over x, y, core).
Axes of the slice: x: 4, y: 4, z: 8, core: 2. Of those that a mesh axis runs over, the one named last changes fastest.
Arguments:
- legendre: float32 [512, 1048576], P('ord', 'grp')
- lon_center: float32 [8], P('grp'), may hold values from 0 to 1
- counts: int32 [8, 32], P('grp'), may hold values from 1 to 4096, 98304 in all within a row
- column_index: int32 [3, 512], replicated, may hold values from 0 to 120, as said below
Outputs:
- factor: float32 [512, 512], replicated
Inputs may be any that keep to these rules, and one draw needn't show every extreme that they name: `column_index`: each column names a different coefficient: row 0 is its degree (at most 120), row 1 its order (at most the degree), row 2 is 1 for a sine term and 0 for a cosine term, and 0 at order 0. Each group's counts add up to 98304.
All inputs are finite; a program needn't handle non-finite values.
Results may differ from a plain program's by a relative error of at most 0.0003.
Values sent between devices are 32-bit elements; how exact they have to be, the bound alone decides.
A program may use at most 64 MiB of HBM per device.

v0:
```python
import math
import jax
import jax.numpy as jnp
from jax import lax
from jax.sharding import PartitionSpec as P

NMAX = 120
quarter_turn = math.pi / 2
track_span = 0.3
kaula_gain = 1.2
highest = lax.Precision.HIGHEST


def upper_factor(matrix):
    return jnp.linalg.cholesky(matrix).T


def block_grams(exchanged):
    blocks = exchanged[:, 0]
    return jnp.einsum("jkb,lkb->kjl", blocks, blocks, precision=highest)


def body(legendre, lon_center, counts, column_index):
    ord_size = lax.axis_size("ord")
    grp_size = lax.axis_size("grp")
    cols_dev, rows_grp = legendre.shape
    rows_dev = rows_grp // ord_size
    scaling = 1.0 / math.sqrt(rows_grp * grp_size)
    own_columns = lax.dynamic_slice_in_dim(
        column_index, lax.axis_index("ord") * cols_dev, cols_dev, 1
    )
    harmonic = own_columns[1].astype(jnp.float32)
    sine_part = own_columns[2].astype(jnp.float32)
    longitude = lon_center[0] + jnp.arange(rows_grp, dtype=jnp.float32) * (track_span / rows_grp)
    harmonic_wave = jnp.cos(
        harmonic[:, None] * longitude[None, :] - sine_part[:, None] * quarter_turn
    )
    slot_index = jnp.arange(rows_dev, dtype=jnp.int32)
    row_valid = (slot_index[None, :] < counts[0][:, None]).astype(jnp.float32).reshape(rows_grp)
    design = legendre * harmonic_wave * (row_valid * scaling)[None, :]
    block_rows = min(512, rows_dev)
    shaped = design.reshape(cols_dev, ord_size, rows_dev // block_rows, block_rows)
    block_gram = block_grams(lax.all_to_all(shaped, "ord", split_axis=1, concat_axis=0, tiled=True))
    local_gram = jnp.sum(block_gram, axis=0)
    degree = column_index[0].astype(jnp.float32)
    kaula_weight = kaula_gain * (degree / NMAX) ** 2
    regular = jnp.diag(kaula_weight * kaula_weight)
    normal = lax.psum(local_gram, ("grp", "ord")) + regular
    return upper_factor(normal)


def solution(mesh):
    placed = (P("ord", "grp"), P("grp"), P("grp", None), P())
    return jax.shard_map(body, mesh=mesh, in_specs=placed, out_specs=P(), check_vma=False)
```

profile of v0, /device:TPU:2, one launch (start us, length us, event | category | flops | bytes accessed | tf_op | source)
XLA Modules:
  0.0 538.6 jit_solution(2535784197587066006)
XLA Ops:
  6.5 0.8 constant_dynamic-slice_fusion
  7.3 0.8 select_bitcast_fusion.1
  8.8 0.2 multiply_add_fusion
  9.0 29.6 %multiply_multiply_fusion = f32[16,131072]{1,0:T(8,128)S(1)} fusion(f32[16,131072]{1,0:T(8,128)} %param.4, f32[131072]{0:T(1024)S(1)} %bitcast.48, f32[16]{0:T(128)S(1)} %multiply_bitcast_fusion, f32[131072]{0:T(1024)S(1)} %multiply_add_fusion, f32[16]{0:T(128)S(1)} %convert_bitcast_fusion), kind=kLoop, calls=%fused_computation | loop fusion | flops 8388608 | bytes 17825920 | tf_op jit(solution)/shard_map/mul | solution.py:40
  38.6 4.9 copy.41
  43.5 20.4 %copy.25 = f32[16,32,8,512]{3,0,2,1:T(8,128)S(1)} copy(f32[16,32,8,512]{3,2,1,0:T(8,128)S(1)} %bitcast.46) | data formatting | bytes 16777216 | tf_op jit(solution)/shard_map/reshape | solution.py:42
  63.8 100.5 %all_to_all.15 = f32[16,32,8,512]{3,0,2,1:T(8,128)S(1)} all-to-all(f32[16,32,8,512]{3,0,2,1:T(8,128)S(1)} %copy.25), channel_id=1, replica_groups=mesh['grp'=8,'ord'=32] {'ord'}, dimensions={1} | all-to-all | bytes 16777216 | tf_op jit(solution)/shard_map/all_to_all | solution.py:43
  164.3 1.9 copy.26
  166.2 16.1 %convolution_bitcast_fusion = f32[512,512]{0,1:T(8,128)} fusion(f32[512,8,512]{2,0,1:T(8,128)S(1)} %bitcast.44), kind=kOutput, calls=%fused_computation.1 | convolution fusion | flops 12884901888 | bytes 9437184 | tf_op jit(solution)/shard_map/jkb,lkb->kjl/dot_general | solution.py:20
  182.4 0.7 multiply_multiply_fusion.1
  183.1 259.9 %all-reduce.3.cloned.1.call-done = f32[512,512]{0,1:T(8,128)} async-done(((f32[512,512]{0,1:T(8,128)}), f32[512,512]{0,1:T(8,128)}) %all-reduce.3.cloned.1.call-update) | async-done | bytes 1048592 | tf_op jit(solution)/shard_map/psum | solution.py:48
  443.0 1.3 select_add_fusion
  444.3 0.3 copy.28
  444.7 1.4 fusion
  446.1 11.7 %cholesky.103 = f32[128,128]{1,0:T(8,128)S(1)} custom-call(f32[128,128]{1,0:T(8,128)S(1)} %cholesky.263), custom_call_target="Cholesky" | custom-call | tf_op jit(solution)/shard_map/jit(cholesky)/cholesky | solution.py:15
  457.9 9.8 %custom-call.27 = f32[1,128,128]{1,2,0:T(8,128)S(1)} custom-call(f32[1,128,128]{2,1,0:T(8,128)S(1)} %get-tuple-element.10), custom_call_target="InvertDiagBlocksLowerTriangular" | custom-call | tf_op jit(solution)/shard_map/jit(cholesky)/cholesky | solution.py:15
  467.7 0.3 fusion.3
  468.0 0.3 convolution_subtract_fusion
  468.4 11.7 %cholesky.215 = f32[128,128]{1,0:T(8,128)S(1)} custom-call(f32[128,128]{1,0:T(8,128)S(1)} %cholesky.267), custom_call_target="Cholesky" | custom-call | tf_op jit(solution)/shard_map/jit(cholesky)/cholesky | solution.py:15
  480.2 0.1 copy.30
  480.5 9.9 %custom-call.28 = f32[1,128,128]{1,2,0:T(8,128)S(1)} custom-call(f32[1,128,128]{2,1,0:T(8,128)S(1)} %get-tuple-element.8), custom_call_target="InvertDiagBlocksLowerTriangular" | custom-call | tf_op jit(solution)/shard_map/jit(cholesky)/cholesky | solution.py:15
  490.6 0.3 convolution_dynamic-update-slice_fusion
  490.9 0.6 convolution_subtract_fusion.1
  491.5 11.7 %cholesky.236 = f32[128,128]{1,0:T(8,128)S(1)} custom-call(f32[128,128]{1,0:T(8,128)S(1)} %cholesky.272), custom_call_target="Cholesky" | custom-call | tf_op jit(solution)/shard_map/jit(cholesky)/cholesky | solution.py:15
  503.4 9.8 %custom-call.29 = f32[1,128,128]{1,2,0:T(8,128)S(1)} custom-call(f32[1,128,128]{2,1,0:T(8,128)S(1)} %get-tuple-element.6), custom_call_target="InvertDiagBlocksLowerTriangular" | custom-call | tf_op jit(solution)/shard_map/jit(cholesky)/cholesky | solution.py:15
  513.2 0.3 convolution_dynamic-update-slice_fusion.1
  513.5 0.5 convolution_subtract_fusion.2
  514.0 11.7 %cholesky.253 = f32[128,128]{1,0:T(8,128)S(1)} custom-call(f32[128,128]{1,0:T(8,128)S(1)} %convolution_subtract_fusion.2), custom_call_target="Cholesky" | custom-call | tf_op jit(solution)/shard_map/jit(cholesky)/cholesky | solution.py:15
  525.8 0.7 compare_reduce_fusion.1
  526.5 0.6 compare_reduce_fusion
  527.2 0.7 compare_reduce_fusion.2
  530.4 1.1 select_bitcast_fusion
  (21 shorter events, 0.8 us)
Async XLA Ops:
  6.5 436.4 %all-reduce.3.cloned.1.call-start = ((), (), s32[]{:S(2)}) async-start(), calls=%async_computation.1 | async-start | bytes 2097152 | tf_op jit(solution)/shard_map/psum | solution.py:48
Sparse Core Ops, SparseCore 0:
  182.5 260.4 all-reduce.2
where the time goes:
time: 542 us; the launch traced here: 539 us
  waiting for transfers between devices  260 us (48%)
  other arithmetic  114 us (21%)
  blocking collectives  100 us (18%)
  local copies, waits for them, and re-layouts  29 us (5%)
  matrix products  18.5 us (3%)
  between operations  17 us (3%)
    psum x1, waiting for transfers between devices, body(): normal = lax.psum(local_gram, ('grp', 'ord')) + regular  260 us
    all_to_all x1, blocking collectives, body(): lax.all_to_all(shaped, 'ord', split_axis=1, concat_axis=0, tiled=True)  100 us
    another operation x14, other arithmetic, upper_factor(): return jnp.linalg.cholesky(matrix).T  78.6 us
    mul x1, other arithmetic, body(): design = legendre * harmonic_wave * (row_valid * scaling)[None, :]  29.6 us
    reshape x1, local copies, waits for them, and re-layouts, body(): design.reshape(cols_dev, ord_size, rows_dev // block_rows, block_rows)  20.4 us
    dot_general x1, matrix products, block_grams(): return jnp.einsum('jkb,lkb->kjl', blocks, blocks, precision=highest)  16.1 us
  transfers between devices with their start and end apart: 1, of which 1 were waited for; matrix products, arithmetic and copies ran while one was open for 0% of the time, Pallas kernels for 0%

commit v1 on v0

--- a/solution.py
+++ b/solution.py
@@ -45,7 +45,7 @@
     degree = column_index[0].astype(jnp.float32)
     kaula_weight = kaula_gain * (degree / NMAX) ** 2
     regular = jnp.diag(kaula_weight * kaula_weight)
-    normal = lax.psum(local_gram, ("grp", "ord")) + regular
+    normal = lax.psum(lax.psum(local_gram, "ord"), "grp") + regular
     return upper_factor(normal)
 
 

time: 542 us -> 477 us (0.88)
  waiting for transfers between devices: 260 us -> 195 us
    psum x1 -> x2, waiting for transfers between devices: 260 us -> 195 us  [body(): normal = lax.psum(lax.psum(local_gram, 'ord'), 'grp') + regular]
  transfers between devices with their start and end apart: 1 -> 2, of which waited for: 1 -> 2; matrix products, arithmetic and copies ran while one was open for 0% -> 0% of each run, Pallas kernels for 0% -> 0%
where the time goes in v1:
time: 477 us; the launch traced here: 473 us
  waiting for transfers between devices  195 us (41%)
  other arithmetic  114 us (24%)
  blocking collectives  100 us (21%)
  local copies, waits for them, and re-layouts  29 us (6%)
  matrix products  18.5 us (4%)
  between operations  17 us (4%)
    psum x2, waiting for transfers between devices, body(): normal = lax.psum(lax.psum(local_gram, 'ord'), 'grp') + regular  195 us
    all_to_all x1, blocking collectives, body(): lax.all_to_all(shaped, 'ord', split_axis=1, concat_axis=0, tiled=True)  100 us
    another operation x14, other arithmetic, upper_factor(): return jnp.linalg.cholesky(matrix).T  78.6 us
    mul x1, other arithmetic, body(): design = legendre * harmonic_wave * (row_valid * scaling)[None, :]  29.6 us
    reshape x1, local copies, waits for them, and re-layouts, body(): design.reshape(cols_dev, ord_size, rows_dev // block_rows, block_rows)  20.4 us
    dot_general x1, matrix products, block_grams(): return jnp.einsum('jkb,lkb->kjl', blocks, blocks, precision=highest)  16.1 us
  transfers between devices with their start and end apart: 2, of which 2 were waited for; matrix products, arithmetic and copies ran while one was open for 0% of the time, Pallas kernels for 0%

profile of v1, /device:TPU:2, one launch (start us, length us, event | category | flops | bytes accessed | tf_op | source)
XLA Modules:
  0.0 473.4 jit_solution(15740051857572074123)
XLA Ops:
  6.5 0.8 constant_dynamic-slice_fusion
  7.3 0.8 select_bitcast_fusion.1
  8.8 0.2 multiply_add_fusion
  9.0 29.6 %multiply_multiply_fusion = f32[16,131072]{1,0:T(8,128)S(1)} fusion(f32[16,131072]{1,0:T(8,128)} %param.4, f32[131072]{0:T(1024)S(1)} %bitcast.48, f32[16]{0:T(128)S(1)} %multiply_bitcast_fusion, f32[131072]{0:T(1024)S(1)} %multiply_add_fusion, f32[16]{0:T(128)S(1)} %convert_bitcast_fusion), kind=kLoop, calls=%fused_computation | loop fusion | flops 8388608 | bytes 17825920 | tf_op jit(solution)/shard_map/mul | solution.py:40
  38.6 4.9 %copy.41 = f32[2,8,256,512]{3,2,1,0:T(8,128)S(1)} copy(f32[2,8,256,512]{3,1,2,0:T(8,128)S(1)} %bitcast.45) | data formatting | bytes 16777216
  43.5 20.4 %copy.25 = f32[16,32,8,512]{3,0,2,1:T(8,128)S(1)} copy(f32[16,32,8,512]{3,2,1,0:T(8,128)S(1)} %bitcast.46) | data formatting | bytes 16777216 | tf_op jit(solution)/shard_map/reshape | solution.py:42
  63.9 100.5 %all_to_all.15 = f32[16,32,8,512]{3,0,2,1:T(8,128)S(1)} all-to-all(f32[16,32,8,512]{3,0,2,1:T(8,128)S(1)} %copy.25), channel_id=1, replica_groups=mesh['grp'=8,'ord'=32] {'ord'}, dimensions={1} | all-to-all | bytes 16777216 | tf_op jit(solution)/shard_map/all_to_all | solution.py:43
  164.3 1.9 copy.26
  166.3 16.1 %convolution_bitcast_fusion = f32[512,512]{0,1:T(8,128)} fusion(f32[512,8,512]{2,0,1:T(8,128)S(1)} %bitcast.44), kind=kOutput, calls=%fused_computation.1 | convolution fusion | flops 12884901888 | bytes 9437184 | tf_op jit(solution)/shard_map/jkb,lkb->kjl/dot_general | solution.py:20
  182.5 116.7 %all-reduce.4.cloned.1.call-done = f32[512,512]{0,1:T(8,128)} async-done(((f32[512,512]{0,1:T(8,128)}), f32[512,512]{0,1:T(8,128)}) %all-reduce.4.cloned.1.call-update) | async-done | bytes 1048592 | tf_op jit(solution)/shard_map/psum | solution.py:48
  299.1 0.7 multiply_multiply_fusion.1
  299.8 78.0 %all-reduce.6.cloned.1.call-done = f32[512,512]{0,1:T(8,128)} async-done(((f32[512,512]{0,1:T(8,128)}), f32[512,512]{0,1:T(8,128)}) %all-reduce.6.cloned.1.call-update) | async-done | bytes 1048592 | tf_op jit(solution)/shard_map/psum | solution.py:48
  377.8 1.3 select_add_fusion
  379.2 0.3 copy.28
  379.5 1.4 fusion
  381.0 11.7 %cholesky.103 = f32[128,128]{1,0:T(8,128)S(1)} custom-call(f32[128,128]{1,0:T(8,128)S(1)} %cholesky.263), custom_call_target="Cholesky" | custom-call | tf_op jit(solution)/shard_map/jit(cholesky)/cholesky | solution.py:15
  392.7 9.8 %custom-call.27 = f32[1,128,128]{1,2,0:T(8,128)S(1)} custom-call(f32[1,128,128]{2,1,0:T(8,128)S(1)} %get-tuple-element.10), custom_call_target="InvertDiagBlocksLowerTriangular" | custom-call | tf_op jit(solution)/shard_map/jit(cholesky)/cholesky | solution.py:15
  402.5 0.3 fusion.3
  402.9 0.3 convolution_subtract_fusion
  403.2 11.7 %cholesky.215 = f32[128,128]{1,0:T(8,128)S(1)} custom-call(f32[128,128]{1,0:T(8,128)S(1)} %cholesky.267), custom_call_target="Cholesky" | custom-call | tf_op jit(solution)/shard_map/jit(cholesky)/cholesky | solution.py:15
  415.3 10.0 %custom-call.28 = f32[1,128,128]{1,2,0:T(8,128)S(1)} custom-call(f32[1,128,128]{2,1,0:T(8,128)S(1)} %get-tuple-element.8), custom_call_target="InvertDiagBlocksLowerTriangular" | custom-call | tf_op jit(solution)/shard_map/jit(cholesky)/cholesky | solution.py:15
  425.4 0.3 convolution_dynamic-update-slice_fusion
  425.8 0.6 convolution_subtract_fusion.1
  426.4 11.7 %cholesky.236 = f32[128,128]{1,0:T(8,128)S(1)} custom-call(f32[128,128]{1,0:T(8,128)S(1)} %cholesky.272), custom_call_target="Cholesky" | custom-call | tf_op jit(solution)/shard_map/jit(cholesky)/cholesky | solution.py:15
  438.2 9.8 %custom-call.29 = f32[1,128,128]{1,2,0:T(8,128)S(1)} custom-call(f32[1,128,128]{2,1,0:T(8,128)S(1)} %get-tuple-element.6), custom_call_target="InvertDiagBlocksLowerTriangular" | custom-call | tf_op jit(solution)/shard_map/jit(cholesky)/cholesky | solution.py:15
  448.0 0.3 convolution_dynamic-update-slice_fusion.1
  448.3 0.5 convolution_subtract_fusion.2
  448.8 11.7 %cholesky.253 = f32[128,128]{1,0:T(8,128)S(1)} custom-call(f32[128,128]{1,0:T(8,128)S(1)} %convolution_subtract_fusion.2), custom_call_target="Cholesky" | custom-call | tf_op jit(solution)/shard_map/jit(cholesky)/cholesky | solution.py:15
  460.7 0.7 compare_reduce_fusion.1
  461.4 0.6 compare_reduce_fusion
  462.0 0.7 compare_reduce_fusion.2
  465.2 1.1 select_bitcast_fusion
  (24 shorter events, 1.0 us)
Async XLA Ops:
  6.5 292.6 %all-reduce.4.cloned.1.call-start = ((), (), s32[]{:S(2)}) async-start(), calls=%async_computation.1 | async-start | bytes 2097152 | tf_op jit(solution)/shard_map/psum | solution.py:48
  182.4 195.4 %all-reduce.6.cloned.1.call-start = ((), (), s32[]{:S(2)}) async-start(), calls=%async_computation.2 | async-start | bytes 2097152 | tf_op jit(solution)/shard_map/psum | solution.py:48
Sparse Core Ops, SparseCore 0:
  182.5 116.5 all-reduce.3
  301.5 76.3 all-reduce.5
